TPU v7x, 256 devices: a whole 4x4x8 slice. The times are simulated.
256 devices in a mesh: seq: 32 (over z, y), head: 8 (over x, core).
Axes of the slice: x: 4, y: 4, z: 8, core: 2. Of those that a mesh axis runs over, the one named last changes fastest.
Arguments:
- queries: bfloat16 [16384, 8192], P('seq', 'head'), may hold values from -6 to 6
- keys: bfloat16 [16384, 8192], P('seq', 'head'), may hold values from -6 to 6
- values: bfloat16 [16384, 8192], P('seq', 'head'), may hold values from -120 to 120
- gate: bfloat16 [16384, 8192], P('seq', 'head'), may hold values from -6 to 6
- grad_out: bfloat16 [16384, 8192], P('seq', 'head'), may hold values from -6 to 6
- gain: float32 [8192], P('head'), may hold values from 0.25 to 1.75
- tile_mask: int32 [128, 4], P('seq'), may hold values from 0 to 1, as said below
Outputs:
- grad_queries: bfloat16 [16384, 8192], P('seq', 'head')
- grad_keys: bfloat16 [16384, 8192], P('seq', 'head')
- grad_values: bfloat16 [16384, 8192], P('seq', 'head')
- grad_gate: bfloat16 [16384, 8192], P('seq', 'head')
- grad_gain: float32 [8192], P('head')
Inputs may be any that keep to these rules, and one draw needn't show every extreme that they name: `tile_mask`: entries are 0 or 1; in every slab's 4 x 4 block the diagonal is 1 and entries above it are 0.
All inputs are finite; a program needn't handle non-finite values.
Results may differ from a plain program's by a relative error of at most 0.0058.
Values sent between devices are 32-bit elements; how exact they have to be, the bound alone decides.
A program may use at most 128 MiB of HBM per device.

v0:
```python
import jax
import jax.numpy as jnp
from jax import lax
from jax.sharding import Mesh
from jax.sharding import PartitionSpec as P

HD = 128
SEQ = ("seq_0", "seq_1")


def filled_with(shard, identity):
    return jnp.zeros_like(shard) + jnp.asarray(identity, shard.dtype)


def prefix_by_axis(shard, axes, combine, identity, reverse):
    before = start = filled_with(shard, identity)
    total = shard
    for axis in reversed(axes):
        count, place = (lax.axis_size(axis), lax.axis_index(axis))
        pieces = lax.all_gather(total, axis)
        inside, total = (start, start)
        for k in reversed(range(count)) if reverse else range(count):
            passed = k > place if reverse else k < place
            total = combine(total, pieces[k])
            inside = jnp.where(passed, total, inside)
        before = combine(inside, before)
    return before


def copy_for_each(shard, axis):
    copies = jnp.broadcast_to(shard, (lax.axis_size(axis), *shard.shape))
    return lax.all_to_all(copies, axis, split_axis=0, concat_axis=0, tiled=True)


def taken_together(shard, axis):
    everything = copy_for_each(shard, axis)
    return jnp.sum(everything, axis=0)


def packed_total(arrays, axis):
    vector, at, done = (jnp.concatenate([a.reshape(-1) for a in arrays]), 0, [])
    total = taken_together(vector, axis)
    for a in arrays:
        done.append(total[at : at + a.size].reshape(a.shape))
        at += a.size
    return tuple(done)


def over_axes(shard, axes):
    for axis in axes:
        shard = lax.psum(shard, axis)
    return shard


def add_states(earlier, later):
    return earlier + later


def keep_mask(tile_rows, rows):
    tiles = tile_rows.shape[0]
    tile_len = rows // tiles
    expand = (
        jnp.broadcast_to(tile_rows[:, None, :, None], (tiles, tile_len, tiles, tile_len)).reshape(
            rows, rows
        )
        == 1
    )
    place = jnp.arange(rows)
    same = place[:, None] // tile_len == place[None, :] // tile_len
    causal = place[:, None] >= place[None, :]
    return expand & (causal | jnp.logical_not(same))


def body(queries, keys, values, gate, grad_out, gain, tile_mask):
    rows, width = queries.shape
    heads_local = width // HD
    bf = jnp.bfloat16
    f = jnp.float32
    q = queries.reshape(rows, heads_local, HD)
    k = keys.reshape(rows, heads_local, HD)
    v = values.reshape(rows, heads_local, HD)
    keep = keep_mask(tile_mask, rows)[None]
    empty = jnp.zeros((heads_local, HD, HD), f)
    local_state = jnp.einsum("the,thf->hef", k, v, preferred_element_type=f)
    prefix = prefix_by_axis(local_state, SEQ, add_states, empty, False)
    prefix_b = prefix.astype(bf)
    scores = jnp.einsum("the,she->hts", q, k, preferred_element_type=f)
    probs = jnp.where(keep, scores, 0.0).astype(bf)
    attn = jnp.einsum("hts,shf->thf", probs, v, preferred_element_type=f)
    attn = attn + jnp.einsum("the,hef->thf", q, prefix_b, preferred_element_type=f)
    flat = attn.reshape(rows, width)
    sig = jax.nn.sigmoid(gate.astype(f))
    upstream = grad_out.astype(f)
    dnorm = upstream * sig
    squares_part = jnp.sum(flat * flat, -1)
    cross_part = jnp.sum(dnorm * gain * flat, -1)
    squares_all, cross_all = packed_total((squares_part, cross_part), "head")
    full_width = width * lax.axis_size("head")
    ms_rows = (squares_all / full_width)[:, None] + 1e-06
    rms = jnp.sqrt(ms_rows)
    normed = flat / rms
    grad_gate = (upstream * normed * gain * sig * (1.0 - sig)).astype(bf)
    grad_gain = over_axes(jnp.sum(dnorm * normed, 0), SEQ)
    cross = (cross_all / full_width)[:, None]
    dattn = ((dnorm * gain - flat * cross / ms_rows) / rms).astype(bf)
    da = dattn.reshape(rows, heads_local, HD)
    local_adj = jnp.einsum("the,thf->hef", q, da, preferred_element_type=f)
    suffix = prefix_by_axis(local_adj, SEQ, add_states, empty, True)
    suffix_b = suffix.astype(bf)
    dprobs = jnp.where(
        keep, jnp.einsum("thf,shf->hts", da, v, preferred_element_type=f), 0.0
    ).astype(bf)
    grad_q = jnp.einsum("hts,she->the", dprobs, k, preferred_element_type=f)
    grad_q = grad_q + jnp.einsum("thf,hef->the", da, prefix_b, preferred_element_type=f)
    grad_k = jnp.einsum("hts,the->she", dprobs, q, preferred_element_type=f)
    grad_k = grad_k + jnp.einsum("shf,hef->she", v, suffix_b, preferred_element_type=f)
    grad_v = jnp.einsum("hts,thf->shf", probs, da, preferred_element_type=f)
    grad_v = grad_v + jnp.einsum("she,hef->shf", k, suffix_b, preferred_element_type=f)
    return (
        grad_q.reshape(rows, width).astype(bf),
        grad_k.reshape(rows, width).astype(bf),
        grad_v.reshape(rows, width).astype(bf),
        grad_gate,
        grad_gain,
    )


def solution(mesh):
    split = Mesh(mesh.devices.reshape(8, 4, mesh.shape["head"]), ("seq_0", "seq_1", "head"))
    return jax.shard_map(
        body,
        mesh=split,
        in_specs=(
            P(SEQ, "head"),
            P(SEQ, "head"),
            P(SEQ, "head"),
            P(SEQ, "head"),
            P(SEQ, "head"),
            P("head"),
            P(SEQ, None),
        ),
        out_specs=(P(SEQ, "head"), P(SEQ, "head"), P(SEQ, "head"), P(SEQ, "head"), P("head")),
        check_vma=False,
    )
```

profile of v0, /device:TPU:1, one launch (start us, length us, event | category | flops | bytes accessed | tf_op | source)
XLA Modules:
  0.0 244.2 jit_solution(2145448634400063631)
XLA Ops:
  7.2 0.0 copy-start
  7.2 0.0 all-gather.11.cloned.1.call-start
  7.2 0.0 copy-start.3
  7.2 2.6 %copy.123 = bf16[64,8,8,128]{3,2,1,0:T(8,128)(2,1)} copy(bf16[64,8,8,128]{3,1,2,0:T(8,128)(2,1)} %bitcast.132) | data formatting | bytes 2097152
  9.8 1.6 copy.90
  11.5 0.0 copy-done.3
  11.5 0.0 copy-start.5
  11.5 1.3 fusion.11
  12.8 0.0 all-gather.11.cloned.1.call-update
  12.8 0.0 all-gather.7.cloned.1.call-start
  12.8 37.1 %all-gather.11.cloned.1.call-done = f32[32,128,128]{2,1,0:T(8,128)} async-done(((f32[8,128,128]{2,1,0:T(8,128)}), f32[32,128,128]{2,1,0:T(8,128)}) %all-gather.11.cloned.1.call-update) | async-done | bytes 2097168 | tf_op jit(solution)/shard_map/all_gather | solution.py:20
  49.9 2.4 fusion.38
  52.3 0.0 copy-done.5
  52.3 0.0 all-gather.7.cloned.1.call-update
  52.3 0.0 all-gather.13.cloned.1.call-start
  52.4 0.0 copy-done.13
  52.5 0.2 broadcast_in_dim.22
  52.7 0.4 fusion.20
  53.0 0.0 copy-start.11
  53.0 0.7 copy-done.11
  53.7 0.0 copy-done
  53.7 2.5 %select_convert_fusion.1 = bf16[8,512,512]{2,1,0:T(8,128)(2,1)S(1)} fusion(pred[512,512]{1,0:T(8,128)(4,1)S(1)} %fusion.20, bf16[512,1024]{1,0:T(8,128)(2,1)} %param.8, bf16[512,1024]{1,0:T(8,128)(2,1)S(1)} %copy-done), kind=kOutput, calls=%fused_computation.1 | convolution fusion | flops 541065216 | bytes 6553600 | tf_op jit(solution)/shard_map/the,she->hts/dot_general | solution.py:87
  56.3 0.0 copy-start.1
  56.3 1.9 copy-done.1
  58.2 2.9 %fusion.6 = f32[8,512,128]{1,2,0:T(8,128)} fusion(bf16[8,512,512]{2,1,0:T(8,128)(2,1)S(1)} %select_convert_fusion.1, bf16[512,1024]{1,0:T(8,128)(2,1)S(1)} %copy-done.3), kind=kOutput, calls=%fused_computation.20 | convolution fusion | flops 536870912 | bytes 7340032 | tf_op jit(solution)/shard_map/hts,shf->thf/dot_general | solution.py:89
  61.1 46.2 %all-gather.7.cloned.1.call-done = f32[8,8,128,128]{3,2,1,0:T(8,128)} async-done(((f32[1,8,128,128]{3,2,1,0:T(8,128)}), f32[8,8,128,128]{3,2,1,0:T(8,128)}) %all-gather.7.cloned.1.call-update) | async-done | bytes 4194320 | tf_op jit(solution)/shard_map/all_gather | solution.py:20
  107.3 3.5 %fusion.37 = bf16[1,8,128,128]{3,2,1,0:T(8,128)(2,1)S(1)} fusion(f32[8,8,128,128]{3,2,1,0:T(8,128)} %all-gather.7.cloned.1.call-done, f32[32,128,128]{2,1,0:T(8,128)} %all-gather.11.cloned.1.call-done, pred[]{:T(512)S(6)} %gt.45, pred[]{:T(512)S(6)} %gt.46, pred[]{:T(512)S(6)} %gt.47, pred[]{:T(512)S(6)} %gt.36, pred[]{:T(512)S(6)} %gt.37, pred[]{:T(512)S(6)} %gt.38, ...), kind=kLoop, calls=%fused_computation.64 | loop fusion | flops 3145728 | bytes 6553612 | tf_op jit(solution)/shard_map/convert_element_type | solution.py:86
  110.7 0.0 copy-done.7
  110.7 1.9 multiply_reduce_fusion.2
  112.6 1.9 copy.96
  114.6 0.0 copy-done.12
  114.6 2.3 multiply_reduce_fusion.1
  116.9 9.6 %all_to_all.6 = f32[8,1,1024]{2,1,0:T(1,128)S(1)} all-to-all(f32[8,1,1024]{2,1,0:T(1,128)S(1)} %broadcast_in_dim.42), channel_id=1, replica_groups=mesh['seq_0'=8,'seq_1'=4,'head'=8] {'head'}, dimensions={0} | all-to-all | bytes 65536 | tf_op jit(solution)/shard_map/all_to_all | solution.py:32
  126.6 4.0 %fusion.3 = (bf16[512,1024]{1,0:T(8,128)(2,1)}, bf16[512,1024]{1,0:T(8,128)(2,1)}, f32[1024]{0:T(1024)S(1)}) fusion(bf16[512,1024]{1,0:T(8,128)(2,1)} %param.11, f32[1024]{0:T(1024)S(1)} %copy-done.12, bf16[512,1024]{1,0:T(8,128)(2,1)} %param.10, f32[512,1024]{1,0:T(8,128)S(1)} %copy.96, f32[512]{0:T(512)S(1)} %get-tuple-element.29, ...), kind=kLoop, calls=%fused_computation.7 | loop fusion | flops 11009024 | bytes 6305792 | tf_op jit(solution)/shard_map/convert_element_type | solution.py:102
  130.6 1.5 copy.118
  132.1 0.5 convolution_bitcast_fusion
  132.5 1.0 copy.104
  133.5 0.0 all-gather.13.cloned.1.call-update
  133.6 0.0 all-gather.9.cloned.1.call-start
  133.6 30.1 %all-gather.13.cloned.1.call-done = f32[32,128,128]{2,1,0:T(8,128)} async-done(((f32[8,128,128]{2,1,0:T(8,128)}), f32[32,128,128]{2,1,0:T(8,128)}) %all-gather.13.cloned.1.call-update) | async-done | bytes 2097168 | tf_op jit(solution)/shard_map/all_gather | solution.py:20
  163.8 2.4 fusion.34
  166.2 0.0 all-gather.9.cloned.1.call-update
  166.2 0.0 copy-start.6
  166.2 2.4 %select_convert_fusion = bf16[8,512,512]{2,1,0:T(8,128)(2,1)S(1)} fusion(pred[512,512]{1,0:T(8,128)(4,1)} %copy-done.11, bf16[512,8,128]{0,2,1:T(8,128)(2,1)S(1)} %bitcast.128, bf16[512,1024]{1,0:T(8,128)(2,1)S(1)} %copy-done.4), kind=kOutput, calls=%fused_computation | convolution fusion | flops 541065216 | bytes 6553600 | tf_op jit(solution)/shard_map/thf,shf->hts/dot_general | solution.py:111
  168.7 0.0 copy-done.6
  168.7 0.0 copy-start.2
  168.7 1.5 fusion.47
  170.2 0.5 copy-done.2
  170.7 1.4 fusion.5
  172.1 2.3 copy.110
  174.3 15.3 %psum.14 = f32[1024]{0:T(1024)S(1)} all-reduce(f32[1024]{0:T(1024)S(1)} %get-tuple-element.27), channel_id=1, replica_groups=mesh['seq_0'=8,'seq_1'=4,'head'=8] {'seq_0'}, use_global_device_ids=true, to_apply=%region_4.5 | all-reduce | flops 1024 | bytes 8192 | tf_op jit(solution)/shard_map/psum | solution.py:51
  189.7 7.8 %psum.15 = f32[1024]{0:T(1024)} all-reduce(f32[1024]{0:T(1024)S(1)} %psum.14), channel_id=1, replica_groups=mesh['seq_0'=8,'seq_1'=4,'head'=8] {'seq_1'}, use_global_device_ids=true, to_apply=%region_5.6 | all-reduce | flops 1024 | bytes 8192 | tf_op jit(solution)/shard_map/psum | solution.py:51
  197.5 4.2 %fusion.48 = f32[8,128,512]{2,1,0:T(8,128)} fusion(bf16[512,8,128]{0,2,1:T(8,128)(2,1)S(1)} %bitcast.130, bf16[8,512,512]{2,1,0:T(8,128)(2,1)} %copy-done.1), kind=kOutput, calls=%fused_computation.94 | convolution fusion | flops 536870912 | bytes 7340032 | tf_op jit(solution)/shard_map/hts,thf->shf/dot_general | solution.py:117
  201.7 19.7 %all-gather.9.cloned.1.call-done = f32[8,8,128,128]{3,2,1,0:T(8,128)} async-done(((f32[1,8,128,128]{3,2,1,0:T(8,128)}), f32[8,8,128,128]{3,2,1,0:T(8,128)}) %all-gather.9.cloned.1.call-update) | async-done | bytes 4194320 | tf_op jit(solution)/shard_map/all_gather | solution.py:20
  221.4 3.4 %fusion.33 = bf16[1,8,128,128]{3,2,1,0:T(8,128)(2,1)S(1)} fusion(f32[8,8,128,128]{3,2,1,0:T(8,128)} %all-gather.9.cloned.1.call-done, f32[32,128,128]{2,1,0:T(8,128)} %all-gather.13.cloned.1.call-done, pred[]{:T(512)S(6)} %lt.45, pred[]{:T(512)S(6)} %lt.46, pred[]{:T(512)S(6)} %lt.47, pred[]{:T(512)S(6)} %lt.36, pred[]{:T(512)S(6)} %lt.37, pred[]{:T(512)S(6)} %lt.38, ...), kind=kLoop, calls=%fused_computation.50 | loop fusion | flops 3145728 | bytes 6553612 | tf_op jit(solution)/shard_map/convert_element_type | solution.py:109
  224.9 0.0 copy-start.8
  224.9 0.0 copy-start.10
  224.9 1.8 fusion.8
  226.7 0.1 copy-done.8
  226.8 0.7 copy-done.10
  227.5 1.5 add_convert_fusion
  229.0 2.4 copy.112
  231.4 4.0 %fusion.4 = bf16[512,8,128]{0,2,1:T(8,128)(2,1)} fusion(f32[8,128,512]{2,1,0:T(8,128)S(1)} %copy-done.9, bf16[8,512,512]{2,1,0:T(8,128)(2,1)} %copy-done.2, bf16[512,1024]{1,0:T(8,128)(2,1)S(1)} %copy-done), kind=kOutput, calls=%fused_computation.9 | convolution fusion | flops 537919488 | bytes 8388608 | tf_op jit(solution)/shard_map/hts,the->she/dot_general | solution.py:115
  235.4 2.3 copy.111
  (13 shorter events, 0.1 us)
Async XLA Ops:
  7.2 46.6 %copy-start = (bf16[512,1024]{1,0:T(8,128)(2,1)S(1)}, bf16[512,1024]{1,0:T(8,128)(2,1)}, u32[]{:S(2)}) copy-start(bf16[512,1024]{1,0:T(8,128)(2,1)} %param.7) | copy-start | bytes 3145732
  7.2 42.7 %all-gather.11.cloned.1.call-start = ((), (), s32[]{:S(2)}) async-start(), calls=%async_computation.3 | async-start | bytes 2621440 | tf_op jit(solution)/shard_map/all_gather | solution.py:20
  7.2 4.3 %copy-start.3 = (bf16[512,1024]{1,0:T(8,128)(2,1)S(1)}, bf16[512,1024]{1,0:T(8,128)(2,1)}, u32[]{:S(2)}) copy-start(bf16[512,1024]{1,0:T(8,128)(2,1)} %param.9) | copy-start | bytes 3145732
  11.5 40.8 %copy-start.5 = (bf16[512,8,128]{0,2,1:T(8,128)(2,1)}, bf16[512,8,128]{0,2,1:T(8,128)(2,1)S(1)}, u32[]{:S(2)}) copy-start(bf16[512,8,128]{0,2,1:T(8,128)(2,1)S(1)} %copy.90) | copy-start | bytes 3145732
  12.8 39.7 %copy-start.13 = (s32[4,4]{1,0:T(4,128)S(1)}, s32[4,4]{1,0:T(4,128)}, u32[]{:S(2)}) copy-start(s32[4,4]{1,0:T(4,128)} %param.13) | copy-start | bytes 196
  12.8 94.5 %all-gather.7.cloned.1.call-start = ((), (), s32[]{:S(2)}) async-start(), calls=%async_computation.1 | async-start | bytes 4718592 | tf_op jit(solution)/shard_map/all_gather | solution.py:20
  52.3 111.4 %all-gather.13.cloned.1.call-start = ((), (), s32[]{:S(2)}) async-start(), calls=%async_computation.4 | async-start | bytes 2621440 | tf_op jit(solution)/shard_map/all_gather | solution.py:20
  53.0 0.7 copy-start.11
  56.3 2.0 copy-start.1
  61.1 49.6 %copy-start.7 = (f32[8,512,128]{1,2,0:T(8,128)S(1)}, f32[8,512,128]{1,2,0:T(8,128)}, u32[]{:S(2)}) copy-start(f32[8,512,128]{1,2,0:T(8,128)} %fusion.6) | copy-start | bytes 6291460
  112.6 1.9 copy-start.12
  133.5 32.7 %copy-start.4 = (bf16[512,1024]{1,0:T(8,128)(2,1)S(1)}, bf16[512,1024]{1,0:T(8,128)(2,1)}, u32[]{:S(2)}) copy-start(bf16[512,1024]{1,0:T(8,128)(2,1)} %param.9) | copy-start | bytes 3145732
  133.6 87.9 %all-gather.9.cloned.1.call-start = ((), (), s32[]{:S(2)}) async-start(), calls=%async_computation.2 | async-start | bytes 4718592 | tf_op jit(solution)/shard_map/all_gather | solution.py:20
  166.2 2.5 %copy-start.6 = (bf16[512,8,128]{0,2,1:T(8,128)(2,1)S(1)}, bf16[512,8,128]{0,2,1:T(8,128)(2,1)}, u32[]{:S(2)}) copy-start(bf16[512,8,128]{0,2,1:T(8,128)(2,1)} %copy-done.5) | copy-start | bytes 3145732
  168.7 2.0 copy-start.2
  224.9 1.9 copy-start.8
  224.9 2.6 %copy-start.10 = (bf16[512,1024]{1,0:T(8,128)(2,1)S(1)}, bf16[512,1024]{1,0:T(8,128)(2,1)}, u32[]{:S(2)}) copy-start(bf16[512,1024]{1,0:T(8,128)(2,1)} %param.8) | copy-start | bytes 3145732
  229.0 2.4 copy-start.9
Sparse Core Ops, SparseCore 0:
  12.9 36.9 all-gather.10
  52.5 54.7 all-gather.6
  133.7 30.0 all-gather.12
  166.3 55.0 all-gather.8
where the time goes:
time: 245 us; the launch traced here: 244 us
  waiting for transfers between devices  133 us (54%)
  blocking collectives  32.7 us (13%)
  matrix products  25.8 us (11%)
  local copies, waits for them, and re-layouts  19.8 us (8%)
  other arithmetic  18.5 us (8%)
  between operations  14 us (6%)
    all_gather x4, waiting for transfers between devices, prefix_by_axis(): pieces = lax.all_gather(total, axis)  133 us
    psum x2, blocking collectives, over_axes(): shard = lax.psum(shard, axis)  23.1 us
    unnamed x32, local copies, waits for them, and re-layouts  13.5 us
    all_to_all x1, blocking collectives, copy_for_each(): return lax.all_to_all(copies, axis, split_axis=0, concat_axis=0, tiled=True)  9.61 us
  transfers between devices with their start and end apart: 4, of which 4 were waited for; matrix products, arithmetic and copies ran while one was open for 7% of the time, Pallas kernels for 0%

commit v1 on v0

v1 whole, which is shorter than its diff:
```python
import functools

import jax
import jax.numpy as jnp
from jax import lax
from jax.experimental import pallas as pl
from jax.experimental.pallas import tpu as pltpu
from jax.sharding import PartitionSpec as P

HD = 128
TILE = 128
NY = 4
CHUNKS = 4
MESH = pl.DeviceIdType.MESH
F32 = jnp.float32
BF = jnp.bfloat16


def dot(a, b):
    return lax.dot_general(a, b, (((1,), (0,)), ((), ())), preferred_element_type=F32)


def dot_nt(a, b):
    return lax.dot_general(a, b, (((1,), (1,)), ((), ())), preferred_element_type=F32)


def dot_tn(a, b):
    return lax.dot_general(a, b, (((0,), (0,)), ((), ())), preferred_element_type=F32)


def each(lo, hi, fn):
    def step(i, carry):
        fn(i)
        return carry

    lax.fori_loop(lo, hi, step, 0)


def layer_kernel(
    nz,
    nh,
    heads,
    rows,
    full,
    q_hbm,
    k_hbm,
    v_hbm,
    gate_hbm,
    go_hbm,
    gain_ref,
    tm_ref,
    gq_hbm,
    gk_hbm,
    gv_hbm,
    gg_hbm,
    gg_sum_ref,
    q,
    k,
    v,
    gate,
    go,
    attn,
    dg,
    da,
    gq,
    gk,
    gv,
    gg,
    gk_in,
    gv_in,
    mask,
    mask_t,
    acc_sq,
    acc_cr,
    rb,
    cb,
    st,
    r1,
    tb,
    r2,
    xb,
    r3,
    pb,
    pr,
    prefb,
    sb,
    hr,
    gp,
    gr1,
    gt,
    gr2,
    in_sem,
    kv_sem,
    out_sem,
    s1,
    v1,
    s2,
    v2,
    s3,
    v3,
    s4,
    v4,
    sh,
    vh,
    sg1,
    vg1,
    sg2,
    vg2,
):
    seq = lax.axis_index("seq")
    head = lax.axis_index("head")
    z = seq // NY
    y = lax.rem(seq, NY)
    per = heads // CHUNKS
    crow = per * HD
    prow = crow // NY
    zrow = prow // nz

    def cols(h):
        return pl.ds(pl.multiple_of(h * HD, HD), HD)

    def ypeer(d):
        yp = lax.rem(y + d, NY)
        return yp, (z * NY + yp, head)

    def zpeer(d):
        zp = lax.rem(z + d, nz)
        return zp, (zp * NY + y, head)

    def hpeer(d):
        return (seq, lax.rem(head + d, nh))

    def rcopy(src, dst, ss, rs, dev):
        return pltpu.make_async_remote_copy(
            src_ref=src, dst_ref=dst, send_sem=ss, recv_sem=rs, device_id=dev, device_id_type=MESH
        )

    bar = pltpu.get_barrier_semaphore()

    def greet(dev):
        pl.semaphore_signal(bar, inc=1, device_id=dev, device_id_type=MESH)

    each(1, NY, lambda d: greet(ypeer(d)[1]))
    each(1, nz, lambda d: greet(zpeer(d)[1]))
    each(1, nh, lambda d: greet(hpeer(d)))

    def kv_copy(c, i):
        src, dst = ((k_hbm, k), (v_hbm, v))[i]
        w = pl.ds(c * crow, crow)
        return pltpu.make_async_copy(src.at[:, w], dst.at[:, w], kv_sem.at[c, i])

    for c in range(CHUNKS):
        kv_copy(c, 0).start()
        kv_copy(c, 1).start()
    loads = [
        pltpu.make_async_copy(a, b, in_sem.at[i])
        for i, (a, b) in enumerate(((q_hbm, q), (go_hbm, go), (gate_hbm, gate)))
    ]
    for cp in loads:
        cp.start()

    def p1(s, c, d):
        yp, dev = ypeer(d)
        src = st.at[s, pl.ds(pl.multiple_of(c * crow + yp * prow, 8), prow)]
        return rcopy(src, r1.at[s, c, y], s1.at[s, c, d - 1], v1.at[s, c, d - 1], dev)

    def p2(s, c, d):
        zp, dev = zpeer(d)
        src = tb.at[s, c, pl.ds(pl.multiple_of(zp * zrow, 8), zrow)]
        return rcopy(src, r2.at[s, c, z], s2.at[s, c, d - 1], v2.at[s, c, d - 1], dev)

    def p3(s, c, d):
        zp, dev = zpeer(d)
        dst = r3.at[s, c, pl.ds(pl.multiple_of(z * zrow, 8), zrow)]
        return rcopy(xb.at[s, c, zp], dst, s3.at[s, c, d - 1], v3.at[s, c, d - 1], dev)

    def p4(s, c, d):
        yp, dev = ypeer(d)
        dst = pr.at[s, pl.ds(pl.multiple_of(c * crow + y * prow, 8), prow)]
        return rcopy(pb.at[s, c, yp], dst, s4.at[s, c, d - 1], v4.at[s, c, d - 1], dev)

    def start_p1(s, c):
        own = st[s, pl.ds(pl.multiple_of(c * crow + y * prow, 8), prow)]
        each(1, NY, lambda d: p1(s, c, d).start())
        r1[s, c, y] = own

    def step_a(s, c):
        each(1, NY, lambda d: p1(s, c, d).wait_recv())
        t = r1[s, c, 0]
        for i in range(1, NY):
            t = t + r1[s, c, i]
        tb[s, c] = t
        each(1, nz, lambda d: p2(s, c, d).start())
        r2[s, c, z] = tb[s, c, pl.ds(pl.multiple_of(z * zrow, 8), zrow)]

    def step_b(s, c):
        each(1, nz, lambda d: p2(s, c, d).wait_recv())
        x = jnp.zeros((zrow, HD), F32)
        for i in range(nz) if s == 0 else reversed(range(nz)):
            xb[s, c, i] = x
            x = x + r2[s, c, i]
        each(1, nz, lambda d: p3(s, c, d).start())
        r3[s, c, pl.ds(pl.multiple_of(z * zrow, 8), zrow)] = xb[s, c, z]

    def step_c(s, c):
        each(1, nz, lambda d: p3(s, c, d).wait_recv())
        x = r3[s, c]
        for i in range(NY) if s == 0 else reversed(range(NY)):
            pb[s, c, i] = x
            x = x + r1[s, c, i]
        each(1, NY, lambda d: p4(s, c, d).start())
        pr[s, pl.ds(pl.multiple_of(c * crow + y * prow, 8), prow)] = pb[s, c, y]

    def wait_d(s, c):
        each(1, NY, lambda d: p4(s, c, d).wait_recv())

    def wait_sends(s):
        def one(c):
            each(1, NY, lambda d: p1(s, c, d).wait_send())
            each(1, nz, lambda d: p2(s, c, d).wait_send())
            each(1, nz, lambda d: p3(s, c, d).wait_send())
            each(1, NY, lambda d: p4(s, c, d).wait_send())

        each(0, CHUNKS, one)

    def state(c):
        def one(h):
            w = cols(h)
            st[0, pl.ds(pl.multiple_of(h * HD, HD), HD)] = dot_tn(k[:, w], v[:, w])

        each(c * per, (c + 1) * per, one)

    for c in range(CHUNKS):
        kv_copy(c, 0).wait()
        kv_copy(c, 1).wait()
        state(c)
        if c == 0:
            pl.semaphore_wait(bar, NY + nz + nh - 3)
        start_p1(0, c)

    tiles = rows // TILE
    at_row = lax.broadcasted_iota(jnp.int32, (TILE, TILE), 0)
    at_col = lax.broadcasted_iota(jnp.int32, (TILE, TILE), 1)
    for i in range(tiles):
        for j in range(tiles):
            on = jnp.full((TILE, TILE), tm_ref[i, j], jnp.int32) == 1
            low = on & (at_row >= at_col) if i == j else on
            high = on & (at_col >= at_row) if i == j else on
            ri, cj = pl.ds(i * TILE, TILE), pl.ds(j * TILE, TILE)
            mask[ri, cj] = jnp.where(low, 1.0, 0.0).astype(BF)
            mask_t[cj, ri] = jnp.where(high, 1.0, 0.0).astype(BF)

    for cp in loads:
        cp.wait()

    half = rows // 2
    lower = ((0, half, half), (half, half, rows))
    upper = ((0, half, 0, rows), (half, half, half, half))

    def fwd(h):
        w = cols(h)
        for r0, rn, cn in lower:
            sc = dot_nt(q[r0 : r0 + rn, w], k[0:cn, w])
            p = sc.astype(BF) * mask[r0 : r0 + rn, 0:cn]
            attn[r0 : r0 + rn, w] = dot(p, v[0:cn, w])
        sig = jax.nn.sigmoid(gate[:, w].astype(F32))
        dg[:, w] = go[:, w].astype(F32) * sig * gain_ref[:, w]

    def finish_attn(h):
        w = cols(h)
        pf = pr[0, pl.ds(pl.multiple_of(h * HD, HD), HD)].astype(BF)
        prefb[h] = pf
        a = attn[:, w] + dot(q[:, w], pf)
        attn[:, w] = a
        acc_sq[...] += a * a
        acc_cr[...] += dg[:, w] * a

    acc_sq[...] = jnp.zeros_like(acc_sq)
    acc_cr[...] = jnp.zeros_like(acc_cr)

    def scan1(i):
        @pl.when(i < heads)
        def _():
            fwd(i)

        @pl.when((i >= 2) & (i < 2 + CHUNKS))
        def _():
            step_a(0, i - 2)

        @pl.when((i >= 5) & (i < 5 + CHUNKS))
        def _():
            step_b(0, i - 5)

        @pl.when((i >= 8) & (i < 8 + CHUNKS))
        def _():
            step_c(0, i - 8)

        @pl.when(i >= 12)
        def _():
            c = i - 12
            wait_d(0, c)
            each(c * per, (c + 1) * per, finish_attn)

    each(0, 12 + CHUNKS, scan1)

    sq_t = jnp.sum(acc_sq[...].T, axis=0, keepdims=True)
    cr_t = jnp.sum(acc_cr[...].T, axis=0, keepdims=True)
    for i in range(tiles):
        sb[i : i + 1] = sq_t[:, i * TILE : (i + 1) * TILE]
        sb[tiles + i : tiles + i + 1] = cr_t[:, i * TILE : (i + 1) * TILE]

    def hx(d):
        return rcopy(sb, hr.at[head], sh.at[d - 1], vh.at[d - 1], hpeer(d))

    each(1, nh, lambda d: hx(d).start())
    hr[head] = sb[...]
    each(1, nh, lambda d: hx(d).wait_recv())
    tot = hr[0]
    for i in range(1, nh):
        tot = tot + hr[i]
    ms = tot[0:tiles] * (1.0 / full) + 1e-06
    inv = 1.0 / jnp.sqrt(ms)
    cross = tot[tiles : 2 * tiles] * (1.0 / full) / ms * inv
    for i in range(tiles):
        rb[i * TILE : (i + 1) * TILE] = jnp.broadcast_to(inv[i : i + 1], (TILE, TILE)).T
        cb[i * TILE : (i + 1) * TILE] = jnp.broadcast_to(cross[i : i + 1], (TILE, TILE)).T

    def adjoint(h):
        w = cols(h)
        d = (dg[:, w] * rb[...] - attn[:, w] * cb[...]).astype(BF)
        da[:, w] = d
        st[1, pl.ds(pl.multiple_of(h * HD, HD), HD)] = dot_tn(q[:, w], d)

    def adj_chunk(c):
        each(c * per, (c + 1) * per, adjoint)
        start_p1(1, c)

    each(0, CHUNKS, adj_chunk)

    def gates(h):
        w = cols(h)
        sig = jax.nn.sigmoid(gate[:, w].astype(F32))
        norm = attn[:, w] * rb[...]
        gg[:, w] = (norm * dg[:, w] * (1.0 - sig)).astype(BF)
        gp[pl.ds(h, 1)] = jnp.sum(go[:, w].astype(F32) * sig * norm, axis=0, keepdims=True)

    def bwd(h):
        w = cols(h)
        pf = prefb[h]
        for r0, rn, cn in lower:
            d = da[r0 : r0 + rn, w]
            dp = dot_nt(d, v[0:cn, w]).astype(BF) * mask[r0 : r0 + rn, 0:cn]
            gq[r0 : r0 + rn, w] = (dot(dp, k[0:cn, w]) + dot_nt(d, pf)).astype(BF)
        for r0, rn, c0, cn in upper:
            d = da[c0 : c0 + cn, w]
            qq = q[c0 : c0 + cn, w]
            m = mask_t[r0 : r0 + rn, c0 : c0 + cn]
            dp = dot_nt(v[r0 : r0 + rn, w], d).astype(BF) * m
            gk_in[r0 : r0 + rn, w] = dot(dp, qq)
            pp = dot_nt(k[r0 : r0 + rn, w], qq).astype(BF) * m
            gv_in[r0 : r0 + rn, w] = dot(pp, d)

    def finish(h):
        w = cols(h)
        sf = pr[1, pl.ds(pl.multiple_of(h * HD, HD), HD)].astype(BF)
        gk[:, w] = (gk_in[:, w] + dot_nt(v[:, w], sf)).astype(BF)
        gv[:, w] = (gv_in[:, w] + dot(k[:, w], sf)).astype(BF)

    def gx1(d):
        return rcopy(gp, gr1.at[y], sg1.at[d - 1], vg1.at[d - 1], ypeer(d)[1])

    def gx2(d):
        return rcopy(gt, gr2.at[z], sg2.at[d - 1], vg2.at[d - 1], zpeer(d)[1])

    outs = ((gq, gq_hbm), (gg, gg_hbm), (gk, gk_hbm), (gv, gv_hbm))

    def out_copy(i, c):
        w = pl.ds(pl.multiple_of(c * crow, crow), crow)
        return pltpu.make_async_copy(outs[i][0].at[:, w], outs[i][1].at[:, w], out_sem.at[i, c])

    def scan2(i):
        @pl.when(i < 4)
        def _():
            each(i * per, (i + 1) * per, gates)
            out_copy(1, i).start()

        @pl.when(i == 3)
        def _():
            each(1, NY, lambda d: gx1(d).start())
            gr1[y] = gp[...]

        @pl.when(i < heads)
        def _():
            bwd(i)

        @pl.when((i < heads) & (lax.rem(i, per) == per - 1))
        def _():
            out_copy(0, i // per).start()

        @pl.when((i >= 1) & (i < 1 + CHUNKS))
        def _():
            step_a(1, i - 1)

        @pl.when((i >= 4) & (i < 4 + CHUNKS))
        def _():
            step_b(1, i - 4)

        @pl.when(i == 6)
        def _():
            each(1, NY, lambda d: gx1(d).wait_recv())
            t = gr1[0]
            for n in range(1, NY):
                t = t + gr1[n]
            gt[...] = t
            each(1, nz, lambda d: gx2(d).start())
            gr2[z] = t

        @pl.when((i >= 7) & (i < 7 + CHUNKS))
        def _():
            step_c(1, i - 7)

        @pl.when(i >= 11)
        def _():
            c = i - 11
            wait_d(1, c)
            each(c * per, (c + 1) * per, finish)
            out_copy(2, c).start()
            out_copy(3, c).start()

    each(0, 11 + CHUNKS, scan2)

    each(1, nz, lambda d: gx2(d).wait_recv())
    t = gr2[0]
    for n in range(1, nz):
        t = t + gr2[n]
    gg_sum_ref[...] = t

    wait_sends(0)
    wait_sends(1)
    each(1, nh, lambda d: hx(d).wait_send())
    each(1, NY, lambda d: gx1(d).wait_send())
    each(1, nz, lambda d: gx2(d).wait_send())
    for i in range(4):
        for c in range(CHUNKS):
            out_copy(i, c).wait()


def body(nz, nh, queries, keys, values, gate, grad_out, gain, tile_mask):
    rows, width = queries.shape
    heads = width // HD
    full = width * nh
    per = heads // CHUNKS
    crow = per * HD
    prow = crow // NY
    zrow = prow // nz
    dma = pltpu.SemaphoreType.DMA
    vm = pltpu.VMEM
    big = jax.ShapeDtypeStruct((rows, width), BF)
    scratch = (
        [vm((rows, width), BF)] * 5
        + [vm((rows, width), F32)] * 2
        + [vm((rows, width), BF)] * 5
        + [vm((rows, width), F32)] * 2
        + [vm((rows, rows), BF)] * 2
        + [vm((rows, HD), F32)] * 4
        + [
            vm((2, heads * HD, HD), F32),
            vm((2, CHUNKS, NY, prow, HD), F32),
            vm((2, CHUNKS, prow, HD), F32),
            vm((2, CHUNKS, nz, zrow, HD), F32),
            vm((2, CHUNKS, nz, zrow, HD), F32),
            vm((2, CHUNKS, prow, HD), F32),
            vm((2, CHUNKS, NY, prow, HD), F32),
            vm((2, heads * HD, HD), F32),
            vm((heads, HD, HD), BF),
            vm((8, HD), F32),
            vm((nh, 8, HD), F32),
            vm((heads, HD), F32),
            vm((NY, heads, HD), F32),
            vm((heads, HD), F32),
            vm((nz, heads, HD), F32),
            dma((3,)),
            dma((CHUNKS, 2)),
            dma((4, CHUNKS)),
            dma((2, CHUNKS, NY - 1)),
            dma((2, CHUNKS, NY - 1)),
            dma((2, CHUNKS, nz - 1)),
            dma((2, CHUNKS, nz - 1)),
            dma((2, CHUNKS, nz - 1)),
            dma((2, CHUNKS, nz - 1)),
            dma((2, CHUNKS, NY - 1)),
            dma((2, CHUNKS, NY - 1)),
            dma((nh - 1,)),
            dma((nh - 1,)),
            dma((NY - 1,)),
            dma((NY - 1,)),
            dma((nz - 1,)),
            dma((nz - 1,)),
        ]
    )
    hbm = pl.BlockSpec(memory_space=pl.ANY)
    out = pl.pallas_call(
        functools.partial(layer_kernel, nz, nh, heads, rows, full),
        out_shape=(big, big, big, big, jax.ShapeDtypeStruct((heads, HD), F32)),
        in_specs=[hbm] * 5
        + [pl.BlockSpec(memory_space=pltpu.VMEM), pl.BlockSpec(memory_space=pltpu.SMEM)],
        out_specs=(hbm, hbm, hbm, hbm, pl.BlockSpec(memory_space=pltpu.VMEM)),
        scratch_shapes=scratch,
        compiler_params=pltpu.CompilerParams(
            collective_id=0, has_side_effects=True, vmem_limit_bytes=60 * 1024 * 1024
        ),
        name="layer",
    )(queries, keys, values, gate, grad_out, gain.reshape(1, width), tile_mask)
    return out[0], out[1], out[2], out[3], out[4].reshape(width)


def solution(mesh):
    nz = mesh.shape["seq"] // NY
    nh = mesh.shape["head"]
    wide = P("seq", "head")
    return jax.shard_map(
        functools.partial(body, nz, nh),
        mesh=mesh,
        in_specs=(wide, wide, wide, wide, wide, P("head"), P("seq", None)),
        out_specs=(wide, wide, wide, wide, P("head")),
        check_vma=False,
    )
```

time: 245 us -> 73.8 us (0.30)
  waiting for transfers between devices: 133 us -> 0 us
  Pallas kernels: 0 us -> 65.5 us
  blocking collectives: 32.7 us -> 0 us
  matrix products: 25.8 us -> 0 us
  other arithmetic: 18.5 us -> 0 us
  between operations: 14 us -> 0.66 us
  local copies, waits for them, and re-layouts: 19.8 us -> 7.13 us
    all_gather x4 -> x0, waiting for transfers between devices: 133 us -> none  [prefix_by_axis(): pieces = lax.all_gather(total, axis)]
    pallas_call x0 -> x1, Pallas kernels: none -> 65.5 us  [body(): pl.pallas_call(functools.partial(layer_kernel, nz, nh, heads, rows, full)...]
    dot_general x12 -> x0, matrix products: 25.8 us -> none  [the longest x1 4.24 us: body(): grad_v = jnp.einsum('hts,thf->shf', probs, da, preferred_element_type=f)]
    psum x2 -> x0, blocking collectives: 23.1 us -> none  [over_axes(): shard = lax.psum(shard, axis)]
    convert_element_type x3 -> x0, other arithmetic: 10.9 us -> none  [the longest x1 4.01 us: body(): grad_gate = (upstream * normed * gain * sig * (1.0 - sig)).astype(bf)]
    all_to_all x1 -> x0, blocking collectives: 9.61 us -> none  [copy_for_each(): return lax.all_to_all(copies, axis, split_axis=0, concat_axis=0, tiled=True)]
    unnamed x32 -> x13, local copies, waits for them, and re-layouts: 13.5 us -> 7.13 us
    reshape x3 -> x0, local copies, waits for them, and re-layouts: 5.05 us -> none  [the longest x1 1.93 us: body(): flat = attn.reshape(rows, width)]
  transfers between devices with their start and end apart: 4 -> 0, of which waited for: 4 -> 0; matrix products, arithmetic and copies ran while one was open for 7% -> 0% of each run, Pallas kernels for 0% -> 0%
where the time goes in v1:
time: 73.8 us; the launch traced here: 73.3 us
  Pallas kernels  65.5 us (89%)
  local copies, waits for them, and re-layouts  7.13 us (10%)
    pallas_call x1, Pallas kernels, body(): pl.pallas_call(functools.partial(layer_kernel, nz, nh, heads, rows, full)...  65.5 us
    unnamed x13, local copies, waits for them, and re-layouts  7.13 us

profile of v1, /device:TPU:1, one launch (start us, length us, event | category | flops | bytes accessed | tf_op | source)
XLA Modules:
  0.0 73.3 jit_solution(5462223196505053395)
XLA Ops:
  0.6 65.5 %layer.1 = (bf16[512,1024]{1,0:T(8,128)(2,1)}, bf16[512,1024]{1,0:T(8,128)(2,1)}, bf16[512,1024]{1,0:T(8,128)(2,1)}, bf16[512,1024]{1,0:T(8,128)(2,1)}, f32[8,128]{1,0:T(8,128)}) custom-call(bf16[512,1024]{1,0:T(8,128)(2,1)} %q_hbm.1, bf16[512,1024]{1,0:T(8,128)(2,1)} %k_hbm.1, bf16[512,1024]{1,0:T(8,128)(2,1)} %v_hbm.1, bf16[512,1024]{1,0:T(8,128)(2,1)} %gate_hbm.1, ...), custom_call_target="tpu_custom_call" | custom-call | tf_op jit(solution)/shard_map/layer/pallas_call | solution.py:502
  66.2 0.0 copy-start.2
  66.2 2.4 %copy.17 = bf16[512,1024]{1,0:T(8,128)(2,1)} copy(bf16[512,1024]{1,0:T(8,128)(2,1)} %get-tuple-element.20) | data formatting | bytes 2097152
  68.5 0.0 copy-done.2
  68.5 0.0 copy-start.1
  68.5 1.0 %copy.18 = bf16[512,1024]{1,0:T(8,128)(2,1)} copy(bf16[512,1024]{1,0:T(8,128)(2,1)S(1)} %copy-done.2) | data formatting | bytes 2097152
  69.5 0.6 copy-done.1
  70.1 0.0 copy-start
  70.1 1.0 %copy.19 = bf16[512,1024]{1,0:T(8,128)(2,1)} copy(bf16[512,1024]{1,0:T(8,128)(2,1)S(1)} %copy-done.1) | data formatting | bytes 2097152
  71.1 0.6 copy-done
  71.7 0.0 copy-start.3
  71.7 1.0 %copy.20 = bf16[512,1024]{1,0:T(8,128)(2,1)} copy(bf16[512,1024]{1,0:T(8,128)(2,1)S(1)} %copy-done) | data formatting | bytes 2097152
  72.7 0.0 copy-done.3
  72.7 0.6 copy.21
Async XLA Ops:
  66.2 2.4 %copy-start.2 = (bf16[512,1024]{1,0:T(8,128)(2,1)S(1)}, bf16[512,1024]{1,0:T(8,128)(2,1)}, u32[]{:S(2)}) copy-start(bf16[512,1024]{1,0:T(8,128)(2,1)} %get-tuple-element.21) | copy-start | bytes 3145732
  68.5 1.6 %copy-start.1 = (bf16[512,1024]{1,0:T(8,128)(2,1)S(1)}, bf16[512,1024]{1,0:T(8,128)(2,1)}, u32[]{:S(2)}) copy-start(bf16[512,1024]{1,0:T(8,128)(2,1)} %get-tuple-element.22) | copy-start | bytes 3145732
  70.1 1.6 %copy-start = (bf16[512,1024]{1,0:T(8,128)(2,1)S(1)}, bf16[512,1024]{1,0:T(8,128)(2,1)}, u32[]{:S(2)}) copy-start(bf16[512,1024]{1,0:T(8,128)(2,1)} %get-tuple-element.23) | copy-start | bytes 3145732
  71.7 1.0 %copy-start.3 = (f32[8,128]{1,0:T(8,128)S(1)}, f32[8,128]{1,0:T(8,128)}, u32[]{:S(2)}) copy-start(f32[8,128]{1,0:T(8,128)} %get-tuple-element.14) | copy-start | bytes 12292

commit v2 on v1

--- a/solution.py
+++ b/solution.py
@@ -34,6 +34,15 @@
         return carry
 
     lax.fori_loop(lo, hi, step, 0)
+
+
+def store_kernel(*refs):
+    sem = refs[10]
+    copies = [pltpu.make_async_copy(refs[i], refs[5 + i], sem.at[i]) for i in range(5)]
+    for cp in copies:
+        cp.start()
+    for cp in copies:
+        cp.wait()
 
 
 def layer_kernel(
@@ -47,12 +56,12 @@
     v_hbm,
     gate_hbm,
     go_hbm,
-    gain_ref,
-    tm_ref,
-    gq_hbm,
-    gk_hbm,
-    gv_hbm,
-    gg_hbm,
+    gain_hbm,
+    tm_hbm,
+    gq,
+    gk,
+    gv,
+    gg,
     gg_sum_ref,
     q,
     k,
@@ -62,10 +71,6 @@
     attn,
     dg,
     da,
-    gq,
-    gk,
-    gv,
-    gg,
     gk_in,
     gv_in,
     mask,
@@ -89,23 +94,14 @@
     gr1,
     gt,
     gr2,
+    gain_ref,
+    tm_ref,
     in_sem,
     kv_sem,
-    out_sem,
-    s1,
-    v1,
-    s2,
-    v2,
-    s3,
-    v3,
-    s4,
-    v4,
-    sh,
-    vh,
-    sg1,
-    vg1,
-    sg2,
-    vg2,
+    sent,
+    came,
+    x_sent,
+    x_came,
 ):
     seq = lax.axis_index("seq")
     head = lax.axis_index("head")
@@ -152,32 +148,36 @@
     for c in range(CHUNKS):
         kv_copy(c, 0).start()
         kv_copy(c, 1).start()
+    pairs = ((tm_hbm, tm_ref), (gain_hbm, gain_ref), (q_hbm, q), (go_hbm, go), (gate_hbm, gate))
     loads = [
         pltpu.make_async_copy(a, b, in_sem.at[i])
-        for i, (a, b) in enumerate(((q_hbm, q), (go_hbm, go), (gate_hbm, gate)))
+        for i, (a, b) in enumerate(pairs)
     ]
     for cp in loads:
         cp.start()
 
+    def settle(ref, sem):
+        pltpu.make_async_copy(ref, ref, sem).wait()
+
     def p1(s, c, d):
         yp, dev = ypeer(d)
         src = st.at[s, pl.ds(pl.multiple_of(c * crow + yp * prow, 8), prow)]
-        return rcopy(src, r1.at[s, c, y], s1.at[s, c, d - 1], v1.at[s, c, d - 1], dev)
+        return rcopy(src, r1.at[s, c, y], sent.at[s, 0], came.at[s, 0, c], dev)
 
     def p2(s, c, d):
         zp, dev = zpeer(d)
         src = tb.at[s, c, pl.ds(pl.multiple_of(zp * zrow, 8), zrow)]
-        return rcopy(src, r2.at[s, c, z], s2.at[s, c, d - 1], v2.at[s, c, d - 1], dev)
+        return rcopy(src, r2.at[s, c, z], sent.at[s, 1], came.at[s, 1, c], dev)
 
     def p3(s, c, d):
         zp, dev = zpeer(d)
         dst = r3.at[s, c, pl.ds(pl.multiple_of(z * zrow, 8), zrow)]
-        return rcopy(xb.at[s, c, zp], dst, s3.at[s, c, d - 1], v3.at[s, c, d - 1], dev)
+        return rcopy(xb.at[s, c, zp], dst, sent.at[s, 2], came.at[s, 2, c], dev)
 
     def p4(s, c, d):
         yp, dev = ypeer(d)
         dst = pr.at[s, pl.ds(pl.multiple_of(c * crow + y * prow, 8), prow)]
-        return rcopy(pb.at[s, c, yp], dst, s4.at[s, c, d - 1], v4.at[s, c, d - 1], dev)
+        return rcopy(pb.at[s, c, yp], dst, sent.at[s, 3], came.at[s, 3, c], dev)
 
     def start_p1(s, c):
         own = st[s, pl.ds(pl.multiple_of(c * crow + y * prow, 8), prow)]
@@ -185,7 +185,7 @@
         r1[s, c, y] = own
 
     def step_a(s, c):
-        each(1, NY, lambda d: p1(s, c, d).wait_recv())
+        settle(r1.at[s, c, 0 : NY - 1], came.at[s, 0, c])
         t = r1[s, c, 0]
         for i in range(1, NY):
             t = t + r1[s, c, i]
@@ -194,7 +194,7 @@
         r2[s, c, z] = tb[s, c, pl.ds(pl.multiple_of(z * zrow, 8), zrow)]
 
     def step_b(s, c):
-        each(1, nz, lambda d: p2(s, c, d).wait_recv())
+        settle(r2.at[s, c, 0 : nz - 1], came.at[s, 1, c])
         x = jnp.zeros((zrow, HD), F32)
         for i in range(nz) if s == 0 else reversed(range(nz)):
             xb[s, c, i] = x
@@ -203,7 +203,7 @@
         r3[s, c, pl.ds(pl.multiple_of(z * zrow, 8), zrow)] = xb[s, c, z]
 
     def step_c(s, c):
-        each(1, nz, lambda d: p3(s, c, d).wait_recv())
+        settle(r3.at[s, c, 0 : (nz - 1) * zrow], came.at[s, 2, c])
         x = r3[s, c]
         for i in range(NY) if s == 0 else reversed(range(NY)):
             pb[s, c, i] = x
@@ -212,16 +212,13 @@
         pr[s, pl.ds(pl.multiple_of(c * crow + y * prow, 8), prow)] = pb[s, c, y]
 
     def wait_d(s, c):
-        each(1, NY, lambda d: p4(s, c, d).wait_recv())
+        settle(pr.at[s, 0 : (NY - 1) * prow], came.at[s, 3, c])
 
     def wait_sends(s):
-        def one(c):
-            each(1, NY, lambda d: p1(s, c, d).wait_send())
-            each(1, nz, lambda d: p2(s, c, d).wait_send())
-            each(1, nz, lambda d: p3(s, c, d).wait_send())
-            each(1, NY, lambda d: p4(s, c, d).wait_send())
-
-        each(0, CHUNKS, one)
+        settle(st.at[s, 0 : CHUNKS * (NY - 1) * prow], sent.at[s, 0])
+        settle(r2.at[s, :, 0 : nz - 1], sent.at[s, 1])
+        settle(xb.at[s, :, 0 : nz - 1], sent.at[s, 2])
+        settle(pb.at[s, :, 0 : NY - 1], sent.at[s, 3])
 
     def state(c):
         def one(h):
@@ -234,23 +231,24 @@
         kv_copy(c, 0).wait()
         kv_copy(c, 1).wait()
         state(c)
-        if c == 0:
-            pl.semaphore_wait(bar, NY + nz + nh - 3)
-        start_p1(0, c)
-
+
+    loads[0].wait()
     tiles = rows // TILE
     at_row = lax.broadcasted_iota(jnp.int32, (TILE, TILE), 0)
     at_col = lax.broadcasted_iota(jnp.int32, (TILE, TILE), 1)
     for i in range(tiles):
         for j in range(tiles):
-            on = jnp.full((TILE, TILE), tm_ref[i, j], jnp.int32) == 1
+            on = jnp.broadcast_to(tm_ref[i : i + 1, j : j + 1], (TILE, TILE)) == 1
             low = on & (at_row >= at_col) if i == j else on
             high = on & (at_col >= at_row) if i == j else on
             ri, cj = pl.ds(i * TILE, TILE), pl.ds(j * TILE, TILE)
             mask[ri, cj] = jnp.where(low, 1.0, 0.0).astype(BF)
             mask_t[cj, ri] = jnp.where(high, 1.0, 0.0).astype(BF)
 
-    for cp in loads:
+    pl.semaphore_wait(bar, NY + nz + nh - 3)
+    each(0, CHUNKS, lambda c: start_p1(0, c))
+
+    for cp in loads[1:]:
         cp.wait()
 
     half = rows // 2
@@ -303,18 +301,19 @@
 
     each(0, 12 + CHUNKS, scan1)
 
-    sq_t = jnp.sum(acc_sq[...].T, axis=0, keepdims=True)
-    cr_t = jnp.sum(acc_cr[...].T, axis=0, keepdims=True)
+    eye = jnp.where(at_row == at_col, 1.0, 0.0)
     for i in range(tiles):
-        sb[i : i + 1] = sq_t[:, i * TILE : (i + 1) * TILE]
-        sb[tiles + i : tiles + i + 1] = cr_t[:, i * TILE : (i + 1) * TILE]
+        ri = slice(i * TILE, (i + 1) * TILE)
+        for n, acc in ((i, acc_sq), (tiles + i, acc_cr)):
+            total = jnp.sum(acc[ri], axis=1, keepdims=True)
+            sb[n : n + 1] = jnp.sum(total * eye, axis=0, keepdims=True)
 
     def hx(d):
-        return rcopy(sb, hr.at[head], sh.at[d - 1], vh.at[d - 1], hpeer(d))
+        return rcopy(sb, hr.at[head], x_sent.at[0], x_came.at[0], hpeer(d))
 
     each(1, nh, lambda d: hx(d).start())
     hr[head] = sb[...]
-    each(1, nh, lambda d: hx(d).wait_recv())
+    settle(hr.at[0 : nh - 1], x_came.at[0])
     tot = hr[0]
     for i in range(1, nh):
         tot = tot + hr[i]
@@ -322,8 +321,10 @@
     inv = 1.0 / jnp.sqrt(ms)
     cross = tot[tiles : 2 * tiles] * (1.0 / full) / ms * inv
     for i in range(tiles):
-        rb[i * TILE : (i + 1) * TILE] = jnp.broadcast_to(inv[i : i + 1], (TILE, TILE)).T
-        cb[i * TILE : (i + 1) * TILE] = jnp.broadcast_to(cross[i : i + 1], (TILE, TILE)).T
+        ri = slice(i * TILE, (i + 1) * TILE)
+        for line, wide in ((inv, rb), (cross, cb)):
+            col = jnp.sum(line[i : i + 1] * eye, axis=1, keepdims=True)
+            wide[ri] = jnp.broadcast_to(col, (TILE, HD))
 
     def adjoint(h):
         w = cols(h)
@@ -367,22 +368,15 @@
         gv[:, w] = (gv_in[:, w] + dot(k[:, w], sf)).astype(BF)
 
     def gx1(d):
-        return rcopy(gp, gr1.at[y], sg1.at[d - 1], vg1.at[d - 1], ypeer(d)[1])
+        return rcopy(gp, gr1.at[y], x_sent.at[1], x_came.at[1], ypeer(d)[1])
 
     def gx2(d):
-        return rcopy(gt, gr2.at[z], sg2.at[d - 1], vg2.at[d - 1], zpeer(d)[1])
-
-    outs = ((gq, gq_hbm), (gg, gg_hbm), (gk, gk_hbm), (gv, gv_hbm))
-
-    def out_copy(i, c):
-        w = pl.ds(pl.multiple_of(c * crow, crow), crow)
-        return pltpu.make_async_copy(outs[i][0].at[:, w], outs[i][1].at[:, w], out_sem.at[i, c])
+        return rcopy(gt, gr2.at[z], x_sent.at[2], x_came.at[2], zpeer(d)[1])
 
     def scan2(i):
         @pl.when(i < 4)
         def _():
             each(i * per, (i + 1) * per, gates)
-            out_copy(1, i).start()
 
         @pl.when(i == 3)
         def _():
@@ -393,10 +387,6 @@
         def _():
             bwd(i)
 
-        @pl.when((i < heads) & (lax.rem(i, per) == per - 1))
-        def _():
-            out_copy(0, i // per).start()
-
         @pl.when((i >= 1) & (i < 1 + CHUNKS))
         def _():
             step_a(1, i - 1)
@@ -407,7 +397,7 @@
 
         @pl.when(i == 6)
         def _():
-            each(1, NY, lambda d: gx1(d).wait_recv())
+            settle(gr1.at[0 : NY - 1], x_came.at[1])
             t = gr1[0]
             for n in range(1, NY):
                 t = t + gr1[n]
@@ -424,12 +414,10 @@
             c = i - 11
             wait_d(1, c)
             each(c * per, (c + 1) * per, finish)
-            out_copy(2, c).start()
-            out_copy(3, c).start()
 
     each(0, 11 + CHUNKS, scan2)
 
-    each(1, nz, lambda d: gx2(d).wait_recv())
+    settle(gr2.at[0 : nz - 1], x_came.at[2])
     t = gr2[0]
     for n in range(1, nz):
         t = t + gr2[n]
@@ -437,12 +425,9 @@
 
     wait_sends(0)
     wait_sends(1)
-    each(1, nh, lambda d: hx(d).wait_send())
-    each(1, NY, lambda d: gx1(d).wait_send())
-    each(1, nz, lambda d: gx2(d).wait_send())
-    for i in range(4):
-        for c in range(CHUNKS):
-            out_copy(i, c).wait()
+    settle(hr.at[0 : nh - 1], x_sent.at[0])
+    settle(gr1.at[0 : NY - 1], x_sent.at[1])
+    settle(gr2.at[0 : nz - 1], x_sent.at[2])
 
 
 def body(nz, nh, queries, keys, values, gate, grad_out, gain, tile_mask):
@@ -459,7 +444,7 @@
     scratch = (
         [vm((rows, width), BF)] * 5
         + [vm((rows, width), F32)] * 2
-        + [vm((rows, width), BF)] * 5
+        + [vm((rows, width), BF)]
         + [vm((rows, width), F32)] * 2
         + [vm((rows, rows), BF)] * 2
         + [vm((rows, HD), F32)] * 4
@@ -479,38 +464,38 @@
             vm((NY, heads, HD), F32),
             vm((heads, HD), F32),
             vm((nz, heads, HD), F32),
+            vm((1, width), F32),
+            vm(tile_mask.shape, jnp.int32),
+            dma((5,)),
+            dma((CHUNKS, 2)),
+            dma((2, 4)),
+            dma((2, 4, CHUNKS)),
             dma((3,)),
-            dma((CHUNKS, 2)),
-            dma((4, CHUNKS)),
-            dma((2, CHUNKS, NY - 1)),
-            dma((2, CHUNKS, NY - 1)),
-            dma((2, CHUNKS, nz - 1)),
-            dma((2, CHUNKS, nz - 1)),
-            dma((2, CHUNKS, nz - 1)),
-            dma((2, CHUNKS, nz - 1)),
-            dma((2, CHUNKS, NY - 1)),
-            dma((2, CHUNKS, NY - 1)),
-            dma((nh - 1,)),
-            dma((nh - 1,)),
-            dma((NY - 1,)),
-            dma((NY - 1,)),
-            dma((nz - 1,)),
-            dma((nz - 1,)),
+            dma((3,)),
         ]
     )
     hbm = pl.BlockSpec(memory_space=pl.ANY)
-    out = pl.pallas_call(
+    args = (queries, keys, values, gate, grad_out, gain.reshape(1, width), tile_mask)
+    parts = pl.pallas_call(
         functools.partial(layer_kernel, nz, nh, heads, rows, full),
         out_shape=(big, big, big, big, jax.ShapeDtypeStruct((heads, HD), F32)),
-        in_specs=[hbm] * 5
-        + [pl.BlockSpec(memory_space=pltpu.VMEM), pl.BlockSpec(memory_space=pltpu.SMEM)],
-        out_specs=(hbm, hbm, hbm, hbm, pl.BlockSpec(memory_space=pltpu.VMEM)),
+        in_specs=[hbm] * 7,
+        out_specs=(pl.BlockSpec(memory_space=pltpu.VMEM),) * 5,
         scratch_shapes=scratch,
         compiler_params=pltpu.CompilerParams(
-            collective_id=0, has_side_effects=True, vmem_limit_bytes=60 * 1024 * 1024
+            collective_id=0, has_side_effects=True, vmem_limit_bytes=36 * 1024 * 1024
         ),
         name="layer",
-    )(queries, keys, values, gate, grad_out, gain.reshape(1, width), tile_mask)
+    )(*(pltpu.with_memory_space_constraint(a, pltpu.HBM) for a in args))
+    out = pl.pallas_call(
+        store_kernel,
+        out_shape=(big, big, big, big, jax.ShapeDtypeStruct((heads, HD), F32)),
+        in_specs=[pl.BlockSpec(memory_space=pltpu.VMEM)] * 5,
+        out_specs=(hbm,) * 5,
+        scratch_shapes=[dma((5,))],
+        compiler_params=pltpu.CompilerParams(vmem_limit_bytes=8 * 1024 * 1024),
+        name="store",
+    )(*parts)
     return out[0], out[1], out[2], out[3], out[4].reshape(width)
 
 

time: 73.8 us -> 63.4 us (0.86)
  local copies, waits for them, and re-layouts: 7.13 us -> 0 us
  Pallas kernels: 65.5 us -> 62.6 us
    unnamed x13 -> x0, local copies, waits for them, and re-layouts: 7.13 us -> none
    pallas_call x1, Pallas kernels: 65.5 us -> 60.6 us  [body(): pl.pallas_call(functools.partial(layer_kernel, nz, nh, heads, rows, full)...]
    pallas_call x0 -> x1, Pallas kernels: none -> 2.05 us  [body(): pl.pallas_call(store_kernel, out_shape=(big, big, big, big, jax.ShapeDtyp...]
where the time goes in v2:
time: 63.4 us; the launch traced here: 63.3 us
  Pallas kernels  62.6 us (99%)
  between operations  0.64 us (1%)
    pallas_call x1, Pallas kernels, body(): pl.pallas_call(functools.partial(layer_kernel, nz, nh, heads, rows, full)...  60.6 us
    pallas_call x1, Pallas kernels, body(): pl.pallas_call(store_kernel, out_shape=(big, big, big, big, jax.ShapeDtyp...  2.05 us

profile of v2, /device:TPU:1, one launch (start us, length us, event | category | flops | bytes accessed | tf_op | source)
XLA Modules:
  0.0 63.3 jit_solution(8056499776259371445)
XLA Ops:
  0.6 60.6 %layer.1 = (bf16[512,1024]{1,0:T(8,128)(2,1)S(1)}, bf16[512,1024]{1,0:T(8,128)(2,1)S(1)}, bf16[512,1024]{1,0:T(8,128)(2,1)S(1)}, bf16[512,1024]{1,0:T(8,128)(2,1)S(1)}, f32[8,128]{1,0:T(8,128)S(1)}) custom-call(bf16[512,1024]{1,0:T(8,128)(2,1)} %q_hbm.1, bf16[512,1024]{1,0:T(8,128)(2,1)} %k_hbm.1, bf16[512,1024]{1,0:T(8,128)(2,1)} %v_hbm.1, ...), custom_call_target="tpu_custom_call" | custom-call | tf_op jit(solution)/shard_map/layer/pallas_call | solution.py:479
  61.2 2.1 %store.1 = (bf16[512,1024]{1,0:T(8,128)(2,1)}, bf16[512,1024]{1,0:T(8,128)(2,1)}, bf16[512,1024]{1,0:T(8,128)(2,1)}, bf16[512,1024]{1,0:T(8,128)(2,1)}, f32[8,128]{1,0:T(8,128)}) custom-call(bf16[512,1024]{1,0:T(8,128)(2,1)S(1)} %get-tuple-element.15.refs_0_, bf16[512,1024]{1,0:T(8,128)(2,1)S(1)} %get-tuple-element.16.refs_1_, ...), custom_call_target="tpu_custom_call" | custom-call | tf_op jit(solution)/shard_map/store/pallas_call | solution.py:490

commit v3 on v2

--- a/solution.py
+++ b/solution.py
@@ -11,6 +11,8 @@
 TILE = 128
 NY = 4
 CHUNKS = 4
+Y_ORDER = (2, 1, 3)
+AHEAD = 4
 MESH = pl.DeviceIdType.MESH
 F32 = jnp.float32
 BF = jnp.bfloat16
@@ -34,6 +36,10 @@
         return carry
 
     lax.fori_loop(lo, hi, step, 0)
+
+
+def far_first(n):
+    return sorted(range(1, n), key=lambda d: -min(d, n - d))
 
 
 def store_kernel(*refs):
@@ -75,6 +81,9 @@
     gv_in,
     mask,
     mask_t,
+    probs_t,
+    dn,
+    slope,
     acc_sq,
     acc_cr,
     rb,
@@ -181,7 +190,8 @@
 
     def start_p1(s, c):
         own = st[s, pl.ds(pl.multiple_of(c * crow + y * prow, 8), prow)]
-        each(1, NY, lambda d: p1(s, c, d).start())
+        for d in Y_ORDER:
+            p1(s, c, d).start()
         r1[s, c, y] = own
 
     def step_a(s, c):
@@ -190,7 +200,8 @@
         for i in range(1, NY):
             t = t + r1[s, c, i]
         tb[s, c] = t
-        each(1, nz, lambda d: p2(s, c, d).start())
+        for d in far_first(nz):
+            p2(s, c, d).start()
         r2[s, c, z] = tb[s, c, pl.ds(pl.multiple_of(z * zrow, 8), zrow)]
 
     def step_b(s, c):
@@ -199,7 +210,8 @@
         for i in range(nz) if s == 0 else reversed(range(nz)):
             xb[s, c, i] = x
             x = x + r2[s, c, i]
-        each(1, nz, lambda d: p3(s, c, d).start())
+        for d in far_first(nz):
+            p3(s, c, d).start()
         r3[s, c, pl.ds(pl.multiple_of(z * zrow, 8), zrow)] = xb[s, c, z]
 
     def step_c(s, c):
@@ -208,7 +220,8 @@
         for i in range(NY) if s == 0 else reversed(range(NY)):
             pb[s, c, i] = x
             x = x + r1[s, c, i]
-        each(1, NY, lambda d: p4(s, c, d).start())
+        for d in Y_ORDER:
+            p4(s, c, d).start()
         pr[s, pl.ds(pl.multiple_of(c * crow + y * prow, 8), prow)] = pb[s, c, y]
 
     def wait_d(s, c):
@@ -261,8 +274,21 @@
             sc = dot_nt(q[r0 : r0 + rn, w], k[0:cn, w])
             p = sc.astype(BF) * mask[r0 : r0 + rn, 0:cn]
             attn[r0 : r0 + rn, w] = dot(p, v[0:cn, w])
+
+    def gated(h):
+        w = cols(h)
         sig = jax.nn.sigmoid(gate[:, w].astype(F32))
-        dg[:, w] = go[:, w].astype(F32) * sig * gain_ref[:, w]
+        d = go[:, w].astype(F32) * sig
+        g = d * gain_ref[:, w]
+        dn[:, w] = d
+        dg[:, w] = g
+        slope[:, w] = g * (1.0 - sig)
+
+    def turned(h):
+        w = cols(h)
+        for r0, rn, c0, cn in upper:
+            pp = dot_nt(k[r0 : r0 + rn, w], q[c0 : c0 + cn, w]).astype(BF)
+            probs_t[h, r0 : r0 + rn, c0 : c0 + cn] = pp * mask_t[r0 : r0 + rn, c0 : c0 + cn]
 
     def finish_attn(h):
         w = cols(h)
@@ -276,30 +302,26 @@
     acc_sq[...] = jnp.zeros_like(acc_sq)
     acc_cr[...] = jnp.zeros_like(acc_cr)
 
+    def during(i, lo, n, fn):
+        @pl.when((i >= lo) & (i < lo + n))
+        def _():
+            fn(i - lo)
+
+    def close1(c):
+        wait_d(0, c)
+        each(c * per, (c + 1) * per, finish_attn)
+
     def scan1(i):
-        @pl.when(i < heads)
-        def _():
-            fwd(i)
-
-        @pl.when((i >= 2) & (i < 2 + CHUNKS))
-        def _():
-            step_a(0, i - 2)
-
-        @pl.when((i >= 5) & (i < 5 + CHUNKS))
-        def _():
-            step_b(0, i - 5)
-
-        @pl.when((i >= 8) & (i < 8 + CHUNKS))
-        def _():
-            step_c(0, i - 8)
-
-        @pl.when(i >= 12)
-        def _():
-            c = i - 12
-            wait_d(0, c)
-            each(c * per, (c + 1) * per, finish_attn)
-
-    each(0, 12 + CHUNKS, scan1)
+        during(i, 0, CHUNKS, lambda c: step_a(0, c))
+        during(i, CHUNKS - 1, CHUNKS, lambda c: step_b(0, c))
+        during(i, 2 * CHUNKS - 2, CHUNKS, lambda c: step_c(0, c))
+        during(i, 0, heads - AHEAD, lambda h: fwd(AHEAD + h))
+        during(i, 0, heads, gated)
+        during(i, 0, heads, turned)
+        during(i, 2 * CHUNKS + 2, CHUNKS, close1)
+
+    each(0, AHEAD, fwd)
+    each(0, 3 * CHUNKS + 2, scan1)
 
     eye = jnp.where(at_row == at_col, 1.0, 0.0)
     for i in range(tiles):
@@ -311,7 +333,8 @@
     def hx(d):
         return rcopy(sb, hr.at[head], x_sent.at[0], x_came.at[0], hpeer(d))
 
-    each(1, nh, lambda d: hx(d).start())
+    for d in far_first(nh):
+        hx(d).start()
     hr[head] = sb[...]
     settle(hr.at[0 : nh - 1], x_came.at[0])
     tot = hr[0]
@@ -340,26 +363,22 @@
 
     def gates(h):
         w = cols(h)
-        sig = jax.nn.sigmoid(gate[:, w].astype(F32))
         norm = attn[:, w] * rb[...]
-        gg[:, w] = (norm * dg[:, w] * (1.0 - sig)).astype(BF)
-        gp[pl.ds(h, 1)] = jnp.sum(go[:, w].astype(F32) * sig * norm, axis=0, keepdims=True)
+        gg[:, w] = (norm * slope[:, w]).astype(BF)
+        gp[pl.ds(h, 1)] = jnp.sum(dn[:, w] * norm, axis=0, keepdims=True)
 
     def bwd(h):
         w = cols(h)
-        pf = prefb[h]
         for r0, rn, cn in lower:
             d = da[r0 : r0 + rn, w]
             dp = dot_nt(d, v[0:cn, w]).astype(BF) * mask[r0 : r0 + rn, 0:cn]
-            gq[r0 : r0 + rn, w] = (dot(dp, k[0:cn, w]) + dot_nt(d, pf)).astype(BF)
+            gq[r0 : r0 + rn, w] = (dot(dp, k[0:cn, w]) + dot_nt(d, prefb[h])).astype(BF)
         for r0, rn, c0, cn in upper:
             d = da[c0 : c0 + cn, w]
-            qq = q[c0 : c0 + cn, w]
             m = mask_t[r0 : r0 + rn, c0 : c0 + cn]
             dp = dot_nt(v[r0 : r0 + rn, w], d).astype(BF) * m
-            gk_in[r0 : r0 + rn, w] = dot(dp, qq)
-            pp = dot_nt(k[r0 : r0 + rn, w], qq).astype(BF) * m
-            gv_in[r0 : r0 + rn, w] = dot(pp, d)
+            gk_in[r0 : r0 + rn, w] = dot(dp, q[c0 : c0 + cn, w])
+            gv_in[r0 : r0 + rn, w] = dot(probs_t[h, r0 : r0 + rn, c0 : c0 + cn], d)
 
     def finish(h):
         w = cols(h)
@@ -373,29 +392,22 @@
     def gx2(d):
         return rcopy(gt, gr2.at[z], x_sent.at[2], x_came.at[2], zpeer(d)[1])
 
+    def close2(c):
+        wait_d(1, c)
+        each(c * per, (c + 1) * per, finish)
+
     def scan2(i):
-        @pl.when(i < 4)
+        during(i, 0, CHUNKS, lambda c: step_a(1, c))
+        during(i, CHUNKS - 1, CHUNKS, lambda c: step_b(1, c))
+        during(i, 2 * CHUNKS - 2, CHUNKS, lambda c: step_c(1, c))
+
+        @pl.when(i == CHUNKS - 1)
         def _():
-            each(i * per, (i + 1) * per, gates)
-
-        @pl.when(i == 3)
-        def _():
+            each(heads // 2, heads, gates)
             each(1, NY, lambda d: gx1(d).start())
             gr1[y] = gp[...]
 
-        @pl.when(i < heads)
-        def _():
-            bwd(i)
-
-        @pl.when((i >= 1) & (i < 1 + CHUNKS))
-        def _():
-            step_a(1, i - 1)
-
-        @pl.when((i >= 4) & (i < 4 + CHUNKS))
-        def _():
-            step_b(1, i - 4)
-
-        @pl.when(i == 6)
+        @pl.when(i == 2 * CHUNKS)
         def _():
             settle(gr1.at[0 : NY - 1], x_came.at[1])
             t = gr1[0]
@@ -405,17 +417,15 @@
             each(1, nz, lambda d: gx2(d).start())
             gr2[z] = t
 
-        @pl.when((i >= 7) & (i < 7 + CHUNKS))
+        @pl.when((i < heads) & (i != CHUNKS - 1))
         def _():
-            step_c(1, i - 7)
-
-        @pl.when(i >= 11)
-        def _():
-            c = i - 11
-            wait_d(1, c)
-            each(c * per, (c + 1) * per, finish)
-
-    each(0, 11 + CHUNKS, scan2)
+            bwd(jnp.where(i < CHUNKS - 1, i + 1, i))
+
+        during(i, 2 * CHUNKS + 2, CHUNKS, close2)
+
+    each(0, heads // 2, gates)
+    bwd(0)
+    each(0, 3 * CHUNKS + 2, scan2)
 
     settle(gr2.at[0 : nz - 1], x_came.at[2])
     t = gr2[0]
@@ -447,6 +457,8 @@
         + [vm((rows, width), BF)]
         + [vm((rows, width), F32)] * 2
         + [vm((rows, rows), BF)] * 2
+        + [vm((heads, rows, rows), BF)]
+        + [vm((rows, width), F32)] * 2
         + [vm((rows, HD), F32)] * 4
         + [
             vm((2, heads * HD, HD), F32),
@@ -483,7 +495,7 @@
         out_specs=(pl.BlockSpec(memory_space=pltpu.VMEM),) * 5,
         scratch_shapes=scratch,
         compiler_params=pltpu.CompilerParams(
-            collective_id=0, has_side_effects=True, vmem_limit_bytes=36 * 1024 * 1024
+            collective_id=0, has_side_effects=True, vmem_limit_bytes=44 * 1024 * 1024
         ),
         name="layer",
     )(*(pltpu.with_memory_space_constraint(a, pltpu.HBM) for a in args))

time: 63.4 us -> 60.2 us (0.950)
  Pallas kernels: 62.6 us -> 58.9 us
    pallas_call x1, Pallas kernels: 60.6 us -> 56.8 us  [body(): pl.pallas_call(functools.partial(layer_kernel, nz, nh, heads, rows, full)...]
where the time goes in v3:
time: 60.2 us; the launch traced here: 59.5 us
  Pallas kernels  58.9 us (98%)
  between operations  0.64 us (1%)
    pallas_call x1, Pallas kernels, body(): pl.pallas_call(functools.partial(layer_kernel, nz, nh, heads, rows, full)...  56.8 us
    pallas_call x1, Pallas kernels, body(): pl.pallas_call(store_kernel, out_shape=(big, big, big, big, jax.ShapeDtyp...  2.05 us

profile of v3, /device:TPU:1, one launch (start us, length us, event | category | flops | bytes accessed | tf_op | source)
XLA Modules:
  0.0 59.5 jit_solution(8125548238638154676)
XLA Ops:
  0.6 56.8 %layer.1 = (bf16[512,1024]{1,0:T(8,128)(2,1)S(1)}, bf16[512,1024]{1,0:T(8,128)(2,1)S(1)}, bf16[512,1024]{1,0:T(8,128)(2,1)S(1)}, bf16[512,1024]{1,0:T(8,128)(2,1)S(1)}, f32[8,128]{1,0:T(8,128)S(1)}) custom-call(bf16[512,1024]{1,0:T(8,128)(2,1)} %q_hbm.1, bf16[512,1024]{1,0:T(8,128)(2,1)} %k_hbm.1, bf16[512,1024]{1,0:T(8,128)(2,1)} %v_hbm.1, ...), custom_call_target="tpu_custom_call" | custom-call | tf_op jit(solution)/shard_map/layer/pallas_call | solution.py:491
  57.5 2.1 %store.1 = (bf16[512,1024]{1,0:T(8,128)(2,1)}, bf16[512,1024]{1,0:T(8,128)(2,1)}, bf16[512,1024]{1,0:T(8,128)(2,1)}, bf16[512,1024]{1,0:T(8,128)(2,1)}, f32[8,128]{1,0:T(8,128)}) custom-call(bf16[512,1024]{1,0:T(8,128)(2,1)S(1)} %get-tuple-element.15.refs_0_, bf16[512,1024]{1,0:T(8,128)(2,1)S(1)} %get-tuple-element.16.refs_1_, ...), custom_call_target="tpu_custom_call" | custom-call | tf_op jit(solution)/shard_map/store/pallas_call | solution.py:502

commit v4 on v3

--- a/solution.py
+++ b/solution.py
@@ -12,6 +12,7 @@
 NY = 4
 CHUNKS = 4
 Y_ORDER = (2, 1, 3)
+SERVED = (2, 1, 7)
 AHEAD = 4
 MESH = pl.DeviceIdType.MESH
 F32 = jnp.float32
@@ -119,7 +120,7 @@
     per = heads // CHUNKS
     crow = per * HD
     prow = crow // NY
-    zrow = prow // nz
+    zrow = prow // (nz // 2)
 
     def cols(h):
         return pl.ds(pl.multiple_of(h * HD, HD), HD)
@@ -168,6 +169,9 @@
     def settle(ref, sem):
         pltpu.make_async_copy(ref, ref, sem).wait()
 
+    def share(i):
+        return pl.ds(pl.multiple_of(lax.rem(i, nz // 2) * zrow, 8), zrow)
+
     def p1(s, c, d):
         yp, dev = ypeer(d)
         src = st.at[s, pl.ds(pl.multiple_of(c * crow + yp * prow, 8), prow)]
@@ -175,12 +179,12 @@
 
     def p2(s, c, d):
         zp, dev = zpeer(d)
-        src = tb.at[s, c, pl.ds(pl.multiple_of(zp * zrow, 8), zrow)]
+        src = tb.at[s, c, share(zp)]
         return rcopy(src, r2.at[s, c, z], sent.at[s, 1], came.at[s, 1, c], dev)
 
     def p3(s, c, d):
         zp, dev = zpeer(d)
-        dst = r3.at[s, c, pl.ds(pl.multiple_of(z * zrow, 8), zrow)]
+        dst = r3.at[s, c, share(z)]
         return rcopy(xb.at[s, c, zp], dst, sent.at[s, 2], came.at[s, 2, c], dev)
 
     def p4(s, c, d):
@@ -202,7 +206,7 @@
         tb[s, c] = t
         for d in far_first(nz):
             p2(s, c, d).start()
-        r2[s, c, z] = tb[s, c, pl.ds(pl.multiple_of(z * zrow, 8), zrow)]
+        r2[s, c, z] = tb[s, c, share(z)]
 
     def step_b(s, c):
         settle(r2.at[s, c, 0 : nz - 1], came.at[s, 1, c])
@@ -210,12 +214,12 @@
         for i in range(nz) if s == 0 else reversed(range(nz)):
             xb[s, c, i] = x
             x = x + r2[s, c, i]
-        for d in far_first(nz):
+        for d in SERVED:
             p3(s, c, d).start()
-        r3[s, c, pl.ds(pl.multiple_of(z * zrow, 8), zrow)] = xb[s, c, z]
+        r3[s, c, share(z)] = xb[s, c, z]
 
     def step_c(s, c):
-        settle(r3.at[s, c, 0 : (nz - 1) * zrow], came.at[s, 2, c])
+        settle(r3.at[s, c, 0 : len(SERVED) * zrow], came.at[s, 2, c])
         x = r3[s, c]
         for i in range(NY) if s == 0 else reversed(range(NY)):
             pb[s, c, i] = x
@@ -230,7 +234,7 @@
     def wait_sends(s):
         settle(st.at[s, 0 : CHUNKS * (NY - 1) * prow], sent.at[s, 0])
         settle(r2.at[s, :, 0 : nz - 1], sent.at[s, 1])
-        settle(xb.at[s, :, 0 : nz - 1], sent.at[s, 2])
+        settle(xb.at[s, :, 0 : len(SERVED)], sent.at[s, 2])
         settle(pb.at[s, :, 0 : NY - 1], sent.at[s, 3])
 
     def state(c):
@@ -447,7 +451,7 @@
     per = heads // CHUNKS
     crow = per * HD
     prow = crow // NY
-    zrow = prow // nz
+    zrow = prow // (nz // 2)
     dma = pltpu.SemaphoreType.DMA
     vm = pltpu.VMEM
     big = jax.ShapeDtypeStruct((rows, width), BF)

time: 60.2 us -> 59.2 us (0.983)
  Pallas kernels: 58.9 us -> 57.8 us
    pallas_call x1, Pallas kernels: 56.8 us -> 55.8 us  [body(): pl.pallas_call(functools.partial(layer_kernel, nz, nh, heads, rows, full)...]
where the time goes in v4:
time: 59.2 us; the launch traced here: 58.5 us
  Pallas kernels  57.8 us (98%)
  between operations  0.64 us (1%)
    pallas_call x1, Pallas kernels, body(): pl.pallas_call(functools.partial(layer_kernel, nz, nh, heads, rows, full)...  55.8 us
    pallas_call x1, Pallas kernels, body(): pl.pallas_call(store_kernel, out_shape=(big, big, big, big, jax.ShapeDtyp...  2.05 us

profile of v4, /device:TPU:1, one launch (start us, length us, event | category | flops | bytes accessed | tf_op | source)
XLA Modules:
  0.0 58.5 jit_solution(9063166733986864974)
XLA Ops:
  0.6 55.8 %layer.1 = (bf16[512,1024]{1,0:T(8,128)(2,1)S(1)}, bf16[512,1024]{1,0:T(8,128)(2,1)S(1)}, bf16[512,1024]{1,0:T(8,128)(2,1)S(1)}, bf16[512,1024]{1,0:T(8,128)(2,1)S(1)}, f32[8,128]{1,0:T(8,128)S(1)}) custom-call(bf16[512,1024]{1,0:T(8,128)(2,1)} %q_hbm.1, bf16[512,1024]{1,0:T(8,128)(2,1)} %k_hbm.1, bf16[512,1024]{1,0:T(8,128)(2,1)} %v_hbm.1, ...), custom_call_target="tpu_custom_call" | custom-call | tf_op jit(solution)/shard_map/layer/pallas_call | solution.py:495
  56.4 2.1 %store.1 = (bf16[512,1024]{1,0:T(8,128)(2,1)}, bf16[512,1024]{1,0:T(8,128)(2,1)}, bf16[512,1024]{1,0:T(8,128)(2,1)}, bf16[512,1024]{1,0:T(8,128)(2,1)}, f32[8,128]{1,0:T(8,128)}) custom-call(bf16[512,1024]{1,0:T(8,128)(2,1)S(1)} %get-tuple-element.15.refs_0_, bf16[512,1024]{1,0:T(8,128)(2,1)S(1)} %get-tuple-element.16.refs_1_, ...), custom_call_target="tpu_custom_call" | custom-call | tf_op jit(solution)/shard_map/store/pallas_call | solution.py:506

commit v5 on v4

--- a/solution.py
+++ b/solution.py
@@ -146,9 +146,12 @@
     def greet(dev):
         pl.semaphore_signal(bar, inc=1, device_id=dev, device_id_type=MESH)
 
-    each(1, NY, lambda d: greet(ypeer(d)[1]))
-    each(1, nz, lambda d: greet(zpeer(d)[1]))
-    each(1, nh, lambda d: greet(hpeer(d)))
+    for d in far_first(nz):
+        greet(zpeer(d)[1])
+    for d in Y_ORDER:
+        greet(ypeer(d)[1])
+    for d in far_first(nh):
+        greet(hpeer(d))
 
     def kv_copy(c, i):
         src, dst = ((k_hbm, k), (v_hbm, v))[i]
@@ -313,7 +316,8 @@
 
     def close1(c):
         wait_d(0, c)
-        each(c * per, (c + 1) * per, finish_attn)
+        for n in range(per):
+            finish_attn(c * per + n)
 
     def scan1(i):
         during(i, 0, CHUNKS, lambda c: step_a(0, c))
@@ -360,7 +364,8 @@
         st[1, pl.ds(pl.multiple_of(h * HD, HD), HD)] = dot_tn(q[:, w], d)
 
     def adj_chunk(c):
-        each(c * per, (c + 1) * per, adjoint)
+        for n in range(per):
+            adjoint(c * per + n)
         start_p1(1, c)
 
     each(0, CHUNKS, adj_chunk)
@@ -398,7 +403,8 @@
 
     def close2(c):
         wait_d(1, c)
-        each(c * per, (c + 1) * per, finish)
+        for n in range(per):
+            finish(c * per + n)
 
     def scan2(i):
         during(i, 0, CHUNKS, lambda c: step_a(1, c))

time: 59.2 us -> 58.9 us (level)
  no operation moved by 1% of the time
where the time goes in v5:
time: 58.9 us; the launch traced here: 58.1 us
  Pallas kernels  57.5 us (98%)
  between operations  0.64 us (1%)
    pallas_call x1, Pallas kernels, body(): pl.pallas_call(functools.partial(layer_kernel, nz, nh, heads, rows, full)...  55.4 us
    pallas_call x1, Pallas kernels, body(): pl.pallas_call(store_kernel, out_shape=(big, big, big, big, jax.ShapeDtyp...  2.05 us

profile of v5, /device:TPU:1, one launch (start us, length us, event | category | flops | bytes accessed | tf_op | source)
XLA Modules:
  0.0 58.1 jit_solution(18419825651150592917)
XLA Ops:
  0.6 55.4 %layer.1 = (bf16[512,1024]{1,0:T(8,128)(2,1)S(1)}, bf16[512,1024]{1,0:T(8,128)(2,1)S(1)}, bf16[512,1024]{1,0:T(8,128)(2,1)S(1)}, bf16[512,1024]{1,0:T(8,128)(2,1)S(1)}, f32[8,128]{1,0:T(8,128)S(1)}) custom-call(bf16[512,1024]{1,0:T(8,128)(2,1)} %q_hbm.1, bf16[512,1024]{1,0:T(8,128)(2,1)} %k_hbm.1, bf16[512,1024]{1,0:T(8,128)(2,1)} %v_hbm.1, ...), custom_call_target="tpu_custom_call" | custom-call | tf_op jit(solution)/shard_map/layer/pallas_call | solution.py:501
  56.0 2.1 %store.1 = (bf16[512,1024]{1,0:T(8,128)(2,1)}, bf16[512,1024]{1,0:T(8,128)(2,1)}, bf16[512,1024]{1,0:T(8,128)(2,1)}, bf16[512,1024]{1,0:T(8,128)(2,1)}, f32[8,128]{1,0:T(8,128)}) custom-call(bf16[512,1024]{1,0:T(8,128)(2,1)S(1)} %get-tuple-element.15.refs_0_, bf16[512,1024]{1,0:T(8,128)(2,1)S(1)} %get-tuple-element.16.refs_1_, ...), custom_call_target="tpu_custom_call" | custom-call | tf_op jit(solution)/shard_map/store/pallas_call | solution.py:512
